TPU v7x, 32 devices: a whole 2x2x4 slice. The times are simulated.
32 devices in a mesh: section: 4 (over x, core), replica: 4 (over z), tensor: 2 (over y).
Axes of the slice: x: 2, y: 2, z: 4, core: 2. Of those that a mesh axis runs over, the one named last changes fastest.
Arguments:
- out_grad: bfloat16 [4, 8, 128, 1024], P('replica', None, 'tensor'), may hold values from -6 to 6
- relu_mask: int32 [4, 4, 8, 128, 4096], P('section', 'replica', None, None, 'tensor'), may hold values from 0 to 255
- w_in: bfloat16 [4, 1024, 32768], P('section', None, 'tensor'), may hold values from -0.1875 to 0.1875
- w_out: bfloat16 [4, 32768, 1024], P('section', 'tensor'), may hold values from -0.03125 to 0.03125
- route: int32 [3, 8, 4], replicated, may hold values from 0 to 3, each once within a row
Outputs:
- in_grads: bfloat16 [4, 4, 8, 128, 1024], P('section', 'replica', None, 'tensor')
Inputs may be any that keep to these rules, and one draw needn't show every extreme that they name: Each route[s, m, :] is a permutation of the replicas.
All inputs are finite; a program needn't handle non-finite values.
Results may differ from a plain program's by a relative error of at most 0.0095.
Values may be sent and summed in bfloat16 or wider, within the bound.
A program may use at most 192 MiB of HBM per device.

v0:
```python
import functools

import jax
import jax.numpy as jnp
from jax import lax
from jax.experimental import pallas as pl
from jax.experimental.pallas import tpu as pltpu
from jax.sharding import PartitionSpec as P

PAIR = 2
BITS = 8
SLOTS = 3
MESH = pl.DeviceIdType.MESH


def relay_kernel(
    sizes, route_ref, grad_ref, mask_ref, w_in_ref, w_out_ref, out_ref,
    kept_out, kept_in, flow_out, flow_in, words_buf, xt, hid_a, hid_b, acc, total,
    parts, shares, peers, arrived, final,
    kept_sem, flow_sem, words_sem, entry_sem, result_sem,
    parts_send, parts_recv, peers_send, peers_recv, relay_send, relay_recv,
):
    n_section, n_replica, n_tensor, groups, pairs, block, chunk = sizes
    section = lax.axis_index("section")
    replica = lax.axis_index("replica")
    tensor = lax.axis_index("tensor")
    last = n_section - 1
    rows, width = final.shape[1:]
    part_rows = rows // PAIR
    tokens = n_tensor * rows
    words = block // BITS
    turns = groups * pairs

    def kept_copies(j):
        start = pl.multiple_of(j * 2 * block, block)
        return (
            pltpu.make_async_copy(w_out_ref.at[pl.ds(start, block), :], kept_out.at[j], kept_sem.at[j, 0]),
            pltpu.make_async_copy(w_in_ref.at[:, pl.ds(start, block)], kept_in.at[j], kept_sem.at[j, 1]),
        )

    def flow_copies(turn):
        slot = lax.rem(turn, SLOTS)
        start = pl.multiple_of((lax.rem(turn, pairs) * 2 + 1) * block, block)
        return (
            pltpu.make_async_copy(w_out_ref.at[pl.ds(start, block), :], flow_out.at[slot], flow_sem.at[slot, 0]),
            pltpu.make_async_copy(w_in_ref.at[:, pl.ds(start, block)], flow_in.at[slot], flow_sem.at[slot, 1]),
        )

    def words_copy(turn):
        slot = lax.rem(turn, SLOTS)
        first = pl.multiple_of(lax.div(turn, pairs) * PAIR, PAIR)
        start = pl.multiple_of(lax.rem(turn, pairs) * 2 * words, 2 * words)
        return pltpu.make_async_copy(
            mask_ref.at[pl.ds(first, PAIR), :, pl.ds(start, 2 * words)], words_buf.at[slot], words_sem.at[slot]
        )

    def parts_copy(g, source, target):
        return pltpu.make_async_remote_copy(
            src_ref=parts.at[g, source], dst_ref=parts.at[g, source],
            send_sem=parts_send.at[g, target], recv_sem=parts_recv.at[g, source],
            device_id=(section, replica, target), device_id_type=MESH,
        )

    def peers_copy(g, source, target):
        return pltpu.make_async_remote_copy(
            src_ref=shares.at[g, target], dst_ref=peers.at[g, source],
            send_sem=peers_send.at[g, target], recv_sem=peers_recv.at[g, source],
            device_id=(section, replica, target), device_id_type=MESH,
        )

    def relay_copy(g, source, to_section, target):
        return pltpu.make_async_remote_copy(
            src_ref=final.at[g], dst_ref=arrived.at[g, source],
            send_sem=relay_send.at[g, target], recv_sem=relay_recv.at[g, source],
            device_id=(to_section, target, tensor), device_id_type=MESH,
        )

    def entry_copy(g):
        return pltpu.make_async_copy(grad_ref.at[g], parts.at[g, tensor], entry_sem.at[g])

    def result_copy(g):
        return pltpu.make_async_copy(final.at[g], out_ref.at[g], result_sem.at[g])

    def others():
        return [lax.rem(tensor + d, n_tensor) for d in range(1, n_tensor)]

    def replicas():
        return [lax.rem(replica + d, n_replica) for d in range(n_replica)]

    def bring(g):
        table = jnp.minimum(section, last - 1)
        for p in range(PAIR):
            picked = jnp.zeros((part_rows, width), jnp.float32)
            for r in range(n_replica):
                chosen = jnp.where(route_ref[table, g * PAIR + p, r] == replica, 1.0, 0.0)
                piece = arrived[g, r, p * part_rows:(p + 1) * part_rows, :]
                picked = picked + chosen * piece.astype(jnp.float32)
            parts[g, tensor, p * part_rows:(p + 1) * part_rows, :] = picked.astype(jnp.bfloat16)
        for peer in others():
            parts_copy(g, tensor, peer).start()

    def receive(g):
        @pl.when(section < last)
        def _():
            for r in range(n_replica):
                relay_copy(g, r, section + 1, r).wait_recv()
            bring(g)

    def finish(g):
        for peer in others():
            peers_copy(g, peer, peer).wait_recv()
        start = pl.multiple_of(tensor * rows, rows)
        summed = total[pl.ds(start, rows), :]
        for peer in others():
            summed = summed + peers[g, peer].astype(jnp.float32)
        final[g] = (parts[g, tensor].astype(jnp.float32) + summed).astype(jnp.bfloat16)
        result_copy(g).start()

        @pl.when(section > 0)
        def _():
            for target in replicas():
                relay_copy(g, replica, section - 1, target).start()

    bit = jnp.left_shift(1, lax.broadcasted_iota(jnp.int32, (1, BITS, tokens), 1))

    def word_rows(slot, half):
        pieces = [
            words_buf[slot, p, t * part_rows:(t + 1) * part_rows, half * words:(half + 1) * words]
            for t in range(n_tensor) for p in range(PAIR)
        ]
        return jnp.concatenate(pieces, axis=0).T

    def half_step(w_out, slot, half, hidden_to, w_in=None, hidden_from=None):
        packed = word_rows(slot, half)
        pieces = block // chunk
        strip = width // pieces
        for c in range(pieces):
            pre = jnp.dot(w_out[c * chunk:(c + 1) * chunk, :], xt[...], preferred_element_type=jnp.float32)
            if w_in is not None:
                acc[c * strip:(c + 1) * strip, :] += jnp.dot(
                    w_in[c * strip:(c + 1) * strip, :], hidden_from[...], preferred_element_type=jnp.float32
                )
            near = packed[c * chunk // BITS:(c + 1) * chunk // BITS]
            keep = (near[:, None, :] & bit) != 0
            hidden = jnp.where(keep, pre.reshape(chunk // BITS, BITS, tokens), 0.0)
            hidden_to[c * chunk:(c + 1) * chunk, :] = hidden.reshape(chunk, tokens).astype(jnp.bfloat16)

    @pl.when(section == last)
    def _():
        for g in range(groups):
            entry_copy(g).start()

    for j in range(pairs):
        for copy in kept_copies(j):
            copy.start()
        if j < 2:
            words_copy(j).start()
            for copy in flow_copies(j):
                copy.start()

    barrier = pltpu.get_barrier_semaphore()
    for peer in others():
        pl.semaphore_signal(barrier, inc=1, device_id=(section, replica, peer), device_id_type=MESH)

    @pl.when(section > 0)
    def _():
        for target in replicas():
            pl.semaphore_signal(barrier, inc=1, device_id=(section - 1, target, tensor), device_id_type=MESH)

    @pl.when(section < last)
    def _():
        for target in replicas():
            pl.semaphore_signal(barrier, inc=1, device_id=(section + 1, target, tensor), device_id_type=MESH)

    greeted = n_tensor - 1
    greeted = greeted + jnp.where(section > 0, n_replica, 0) + jnp.where(section < last, n_replica, 0)
    pl.semaphore_wait(barrier, greeted)

    @pl.when(section == last)
    def _():
        for g in range(groups):
            entry_copy(g).wait()
            for peer in others():
                parts_copy(g, tensor, peer).start()

    receive(0)
    finish_at = min(1, pairs - 1)
    receive_at = max(pairs - 2, 0)

    @pl.loop(0, groups)
    def _(g):
        for peer in others():
            parts_copy(g, peer, peer).wait_recv()
        xt[...] = parts[g].reshape(tokens, width).T
        acc[...] = jnp.zeros_like(acc)

        @pl.loop(0, pairs)
        def _(j):
            turn = g * pairs + j
            slot = lax.rem(turn, SLOTS)
            before = lax.rem(turn + SLOTS - 1, SLOTS)
            words_copy(turn).wait()

            @pl.when(g == 0)
            def _():
                for copy in kept_copies(j):
                    copy.wait()

            @pl.when(j == 0)
            def _():
                half_step(kept_out.at[j], slot, 0, hid_a)

            @pl.when(j > 0)
            def _():
                half_step(kept_out.at[j], slot, 0, hid_a, flow_in.at[before], hid_b)

            @pl.when(turn + 2 < turns)
            def _():
                words_copy(turn + 2).start()
                for copy in flow_copies(turn + 2):
                    copy.start()

            for copy in flow_copies(turn):
                copy.wait()
            half_step(flow_out.at[slot], slot, 1, hid_b, kept_in.at[j], hid_a)

            @pl.when((j == finish_at) & (g > 0))
            def _():
                finish(g - 1)

            @pl.when((j == receive_at) & (g + 1 < groups))
            def _():
                receive(g + 1)

        final_slot = lax.rem(g * pairs + pairs - 1, SLOTS)
        acc[...] += jnp.dot(flow_in[final_slot], hid_b[...], preferred_element_type=jnp.float32)
        total[...] = acc[...].T
        shares[g] = total[...].reshape(n_tensor, rows, width).astype(jnp.bfloat16)
        for peer in others():
            peers_copy(g, tensor, peer).start()

    finish(groups - 1)

    for g in range(groups):
        result_copy(g).wait()
        for peer in others():
            parts_copy(g, tensor, peer).wait_send()
            peers_copy(g, tensor, peer).wait_send()

    @pl.when(section > 0)
    def _():
        for g in range(groups):
            for target in replicas():
                relay_copy(g, replica, section - 1, target).wait_send()


def shards(out_grad, relu_mask, w_in, w_out, route):
    n_section = lax.axis_size("section")
    n_replica = lax.axis_size("replica")
    n_tensor = lax.axis_size("tensor")
    micro, part_rows, width = out_grad.shape[1:]
    units = w_out.shape[1]
    groups = micro // PAIR
    rows = PAIR * part_rows
    tokens = n_tensor * rows
    block = min(1024, units // 2)
    chunk = block // 1
    pairs = units // (2 * block)
    words = block // BITS
    bf16, f32, dma = jnp.bfloat16, jnp.float32, pltpu.SemaphoreType.DMA
    sizes = (n_section, n_replica, n_tensor, groups, pairs, block, chunk)
    hbm = pl.BlockSpec(memory_space=pl.ANY)
    results = pl.pallas_call(
        functools.partial(relay_kernel, sizes),
        out_shape=jax.ShapeDtypeStruct((groups, rows, width), bf16),
        in_specs=[pl.BlockSpec(memory_space=pltpu.SMEM), hbm, hbm, hbm, hbm],
        out_specs=hbm,
        scratch_shapes=[
            pltpu.VMEM((pairs, block, width), bf16),
            pltpu.VMEM((pairs, width, block), bf16),
            pltpu.VMEM((SLOTS, block, width), bf16),
            pltpu.VMEM((SLOTS, width, block), bf16),
            pltpu.VMEM((SLOTS, PAIR, n_tensor * part_rows, 2 * words), jnp.int32),
            pltpu.VMEM((width, tokens), bf16),
            pltpu.VMEM((block, tokens), bf16),
            pltpu.VMEM((block, tokens), bf16),
            pltpu.VMEM((width, tokens), f32),
            pltpu.VMEM((tokens, width), f32),
            pltpu.VMEM((groups, n_tensor, rows, width), bf16),
            pltpu.VMEM((groups, n_tensor, rows, width), bf16),
            pltpu.VMEM((groups, n_tensor, rows, width), bf16),
            pltpu.VMEM((groups, n_replica, rows, width), bf16),
            pltpu.VMEM((groups, rows, width), bf16),
            dma((pairs, 2)), dma((SLOTS, 2)), dma((SLOTS,)), dma((groups,)), dma((groups,)),
            dma((groups, n_tensor)), dma((groups, n_tensor)),
            dma((groups, n_tensor)), dma((groups, n_tensor)),
            dma((groups, n_replica)), dma((groups, n_replica)),
        ],
        compiler_params=pltpu.CompilerParams(
            collective_id=0, has_side_effects=True, vmem_limit_bytes=67043328
        ),
        name="relay",
    )(route, out_grad.reshape(groups, rows, width), relu_mask[0, 0], w_in[0], w_out[0])
    return results.reshape(micro, part_rows, width)[None, None]


def solution(mesh):
    in_specs = (
        P("replica", None, "tensor", None),
        P("section", "replica", None, None, "tensor"),
        P("section", None, "tensor"),
        P("section", "tensor", None),
        P(),
    )
    out_specs = P("section", "replica", None, "tensor", None)
    return jax.shard_map(shards, mesh=mesh, in_specs=in_specs, out_specs=out_specs, check_vma=False)
```

profile of v0, /device:TPU:0, one launch (start us, length us, event | category | flops | bytes accessed | tf_op | source)
XLA Modules:
  0.0 265.8 jit_solution(9757948313468798547)
XLA Ops:
  0.0 1.4 copy.6.route_ref
  1.4 262.1 %relay.1 = bf16[4,128,1024]{2,1,0:T(8,128)(2,1)} custom-call(s32[3,8,4]{2,1,0:T(8,128)} %copy.6.route_ref, bf16[4,128,1024]{2,1,0:T(8,128)(2,1)} %bitcast.9, s32[8,128,2048]{2,1,0:T(8,128)} %bitcast.7, bf16[1024,16384]{1,0:T(8,128)(2,1)} %bitcast.5, bf16[16384,1024]{1,0:T(8,128)(2,1)} %bitcast.6), custom_call_target="tpu_custom_call" | custom-call | tf_op jit(solution)/shard_map/relay/pallas_call | solution.py:273
  263.5 2.3 copy.8
where the time goes:
time: 270 us; the launch traced here: 266 us
  Pallas kernels  262 us (97%)
  local copies, waits for them, and re-layouts  3.64 us (1%)
    pallas_call x1, Pallas kernels, shards(): pl.pallas_call(functools.partial(relay_kernel, sizes), out_shape=jax.Shap...  262 us

commit v1 on v0

--- a/solution.py
+++ b/solution.py
@@ -16,9 +16,9 @@
 def relay_kernel(
     sizes, route_ref, grad_ref, mask_ref, w_in_ref, w_out_ref, out_ref,
     kept_out, kept_in, flow_out, flow_in, words_buf, xt, hid_a, hid_b, acc, total,
-    parts, shares, peers, arrived, final,
+    parts, shares, peers, arrived, final, forward,
     kept_sem, flow_sem, words_sem, entry_sem, result_sem,
-    parts_send, parts_recv, peers_send, peers_recv, relay_send, relay_recv,
+    parts_send, parts_recv, peers_send, peers_recv, relay_send, relay_recv, forward_send,
 ):
     n_section, n_replica, n_tensor, groups, pairs, block, chunk = sizes
     section = lax.axis_index("section")
@@ -54,26 +54,49 @@
             mask_ref.at[pl.ds(first, PAIR), :, pl.ds(start, 2 * words)], words_buf.at[slot], words_sem.at[slot]
         )
 
-    def parts_copy(g, source, target):
+    bridged = n_replica == 4
+
+    def band(p):
+        return pl.ds(p * part_rows, part_rows)
+
+    def parts_copy(g, p, source, target):
         return pltpu.make_async_remote_copy(
-            src_ref=parts.at[g, source], dst_ref=parts.at[g, source],
-            send_sem=parts_send.at[g, target], recv_sem=parts_recv.at[g, source],
+            src_ref=parts.at[g, source, band(p), :], dst_ref=parts.at[g, source, band(p), :],
+            send_sem=parts_send.at[g, p, target], recv_sem=parts_recv.at[g, p, source],
             device_id=(section, replica, target), device_id_type=MESH,
         )
 
-    def peers_copy(g, source, target):
+    def peers_copy(g, p, source, target):
         return pltpu.make_async_remote_copy(
-            src_ref=shares.at[g, target], dst_ref=peers.at[g, source],
-            send_sem=peers_send.at[g, target], recv_sem=peers_recv.at[g, source],
+            src_ref=shares.at[g, target, band(p), :], dst_ref=peers.at[g, source, band(p), :],
+            send_sem=peers_send.at[g, p, target], recv_sem=peers_recv.at[g, p, source],
             device_id=(section, replica, target), device_id_type=MESH,
         )
 
-    def relay_copy(g, source, to_section, target):
+    def relay_copy(g, p, i, source, to_section, target):
         return pltpu.make_async_remote_copy(
-            src_ref=final.at[g], dst_ref=arrived.at[g, source],
-            send_sem=relay_send.at[g, target], recv_sem=relay_recv.at[g, source],
+            src_ref=final.at[g, band(p), :], dst_ref=arrived.at[g, source, band(p), :],
+            send_sem=relay_send.at[g, p, i], recv_sem=relay_recv.at[g, p, source],
             device_id=(to_section, target, tensor), device_id_type=MESH,
         )
+
+    def forward_copy(g, p, slot, target):
+        return pltpu.make_async_remote_copy(
+            src_ref=forward.at[g, band(p), :], dst_ref=arrived.at[g, slot, band(p), :],
+            send_sem=forward_send.at[g, p], recv_sem=relay_recv.at[g, p, slot],
+            device_id=(section, target, tensor), device_id_type=MESH,
+        )
+
+    if bridged:
+        low = replica < 2
+        inner = (replica == 1) | (replica == 2)
+        partner = jnp.where(lax.rem(replica, 2) == 0, replica + 1, replica - 1)
+        far = jnp.where(low, 2, 0)
+        far_slot = jnp.where(low, 2, 1)
+        targets = [jnp.int32(1), jnp.int32(2), jnp.where(low, 0, 3)]
+    else:
+        inner = True
+        targets = [lax.rem(replica + d, n_replica) for d in range(n_replica)]
 
     def entry_copy(g):
         return pltpu.make_async_copy(grad_ref.at[g], parts.at[g, tensor], entry_sem.at[g])
@@ -84,42 +107,70 @@
     def others():
         return [lax.rem(tensor + d, n_tensor) for d in range(1, n_tensor)]
 
-    def replicas():
-        return [lax.rem(replica + d, n_replica) for d in range(n_replica)]
-
-    def bring(g):
-        table = jnp.minimum(section, last - 1)
-        for p in range(PAIR):
-            picked = jnp.zeros((part_rows, width), jnp.float32)
-            for r in range(n_replica):
-                chosen = jnp.where(route_ref[table, g * PAIR + p, r] == replica, 1.0, 0.0)
-                piece = arrived[g, r, p * part_rows:(p + 1) * part_rows, :]
-                picked = picked + chosen * piece.astype(jnp.float32)
-            parts[g, tensor, p * part_rows:(p + 1) * part_rows, :] = picked.astype(jnp.bfloat16)
-        for peer in others():
-            parts_copy(g, tensor, peer).start()
-
-    def receive(g):
-        @pl.when(section < last)
+    table = jnp.minimum(section, last - 1)
+
+    def gathered(g, p, terms, target):
+        picked = jnp.zeros((part_rows, width), jnp.float32)
+        for slot, sources in terms:
+            chosen = 0.0
+            for r in sources:
+                chosen = chosen + jnp.where(route_ref[table, g * PAIR + p, r] == target, 1.0, 0.0)
+            picked = picked + chosen * arrived[g, slot, band(p), :].astype(jnp.float32)
+        return picked.astype(jnp.bfloat16)
+
+    def land(g, p, slot):
+        relay_copy(g, p, 0, slot, section, replica).wait_recv()
+
+    def pass_on(g, p):
+        if not bridged:
+            return
+
+        @pl.when((section < last) & inner)
         def _():
             for r in range(n_replica):
-                relay_copy(g, r, section + 1, r).wait_recv()
-            bring(g)
-
-    def finish(g):
+                land(g, p, r)
+            forward[g, band(p), :] = gathered(g, p, [(far, [far]), (far + 1, [far + 1])], partner)
+            forward_copy(g, p, far_slot, partner).start()
+
+    def bring(g, p):
+        def give():
+            for peer in others():
+                parts_copy(g, p, tensor, peer).start()
+
+        @pl.when((section < last) & inner)
+        def _():
+            if not bridged:
+                for r in range(n_replica):
+                    land(g, p, r)
+            parts[g, tensor, band(p), :] = gathered(g, p, [(r, [r]) for r in range(n_replica)], replica)
+            give()
+
+        if bridged:
+            @pl.when((section < last) & jnp.logical_not(inner))
+            def _():
+                for slot in (replica, partner, far_slot):
+                    land(g, p, slot)
+                parts[g, tensor, band(p), :] = gathered(
+                    g, p, [(replica, [replica]), (partner, [partner]), (far_slot, [far, far + 1])], replica
+                )
+                give()
+
+    def finish(g, p):
         for peer in others():
-            peers_copy(g, peer, peer).wait_recv()
-        start = pl.multiple_of(tensor * rows, rows)
-        summed = total[pl.ds(start, rows), :]
+            peers_copy(g, p, peer, peer).wait_recv()
+        start = pl.multiple_of(tensor * rows + p * part_rows, part_rows)
+        summed = total[pl.ds(start, part_rows), :]
         for peer in others():
-            summed = summed + peers[g, peer].astype(jnp.float32)
-        final[g] = (parts[g, tensor].astype(jnp.float32) + summed).astype(jnp.bfloat16)
-        result_copy(g).start()
+            summed = summed + peers[g, peer, band(p), :].astype(jnp.float32)
+        final[g, band(p), :] = (parts[g, tensor, band(p), :].astype(jnp.float32) + summed).astype(jnp.bfloat16)
 
         @pl.when(section > 0)
         def _():
-            for target in replicas():
-                relay_copy(g, replica, section - 1, target).start()
+            for i, target in enumerate(targets):
+                relay_copy(g, p, i, replica, section - 1, target).start()
+
+        if p == PAIR - 1:
+            result_copy(g).start()
 
     bit = jnp.left_shift(1, lax.broadcasted_iota(jnp.int32, (1, BITS, tokens), 1))
 
@@ -159,20 +210,22 @@
                 copy.start()
 
     barrier = pltpu.get_barrier_semaphore()
+    if bridged:
+        pl.semaphore_signal(barrier, inc=1, device_id=(section, partner, tensor), device_id_type=MESH)
     for peer in others():
         pl.semaphore_signal(barrier, inc=1, device_id=(section, replica, peer), device_id_type=MESH)
 
     @pl.when(section > 0)
     def _():
-        for target in replicas():
+        for target in range(n_replica):
             pl.semaphore_signal(barrier, inc=1, device_id=(section - 1, target, tensor), device_id_type=MESH)
 
     @pl.when(section < last)
     def _():
-        for target in replicas():
+        for target in range(n_replica):
             pl.semaphore_signal(barrier, inc=1, device_id=(section + 1, target, tensor), device_id_type=MESH)
 
-    greeted = n_tensor - 1
+    greeted = n_tensor - 1 + (1 if bridged else 0)
     greeted = greeted + jnp.where(section > 0, n_replica, 0) + jnp.where(section < last, n_replica, 0)
     pl.semaphore_wait(barrier, greeted)
 
@@ -180,17 +233,23 @@
     def _():
         for g in range(groups):
             entry_copy(g).wait()
-            for peer in others():
-                parts_copy(g, tensor, peer).start()
-
-    receive(0)
-    finish_at = min(1, pairs - 1)
-    receive_at = max(pairs - 2, 0)
+            for p in range(PAIR):
+                for peer in others():
+                    parts_copy(g, p, tensor, peer).start()
+
+    for p in range(PAIR):
+        pass_on(0, p)
+    for p in range(PAIR):
+        bring(0, p)
+    finish_at = [min(p, pairs - 1) for p in range(PAIR)]
+    pass_at = [max(pairs - 2 - PAIR + p, 0) for p in range(PAIR)]
+    bring_at = [max(pairs - 1 - PAIR + p, 0) for p in range(PAIR)]
 
     @pl.loop(0, groups)
     def _(g):
-        for peer in others():
-            parts_copy(g, peer, peer).wait_recv()
+        for p in range(PAIR):
+            for peer in others():
+                parts_copy(g, p, peer, peer).wait_recv()
         xt[...] = parts[g].reshape(tokens, width).T
         acc[...] = jnp.zeros_like(acc)
 
@@ -224,34 +283,52 @@
                 copy.wait()
             half_step(flow_out.at[slot], slot, 1, hid_b, kept_in.at[j], hid_a)
 
-            @pl.when((j == finish_at) & (g > 0))
-            def _():
-                finish(g - 1)
-
-            @pl.when((j == receive_at) & (g + 1 < groups))
-            def _():
-                receive(g + 1)
+            for p in range(PAIR):
+                @pl.when((j == finish_at[p]) & (g > 0))
+                def _():
+                    finish(g - 1, p)
+
+            for p in range(PAIR):
+                @pl.when((j == pass_at[p]) & (g + 1 < groups))
+                def _():
+                    pass_on(g + 1, p)
+
+            for p in range(PAIR):
+                @pl.when((j == bring_at[p]) & (g + 1 < groups))
+                def _():
+                    bring(g + 1, p)
 
         final_slot = lax.rem(g * pairs + pairs - 1, SLOTS)
         acc[...] += jnp.dot(flow_in[final_slot], hid_b[...], preferred_element_type=jnp.float32)
         total[...] = acc[...].T
         shares[g] = total[...].reshape(n_tensor, rows, width).astype(jnp.bfloat16)
-        for peer in others():
-            peers_copy(g, tensor, peer).start()
-
-    finish(groups - 1)
+        for p in range(PAIR):
+            for peer in others():
+                peers_copy(g, p, tensor, peer).start()
+
+    for p in range(PAIR):
+        finish(groups - 1, p)
 
     for g in range(groups):
         result_copy(g).wait()
-        for peer in others():
-            parts_copy(g, tensor, peer).wait_send()
-            peers_copy(g, tensor, peer).wait_send()
+        for p in range(PAIR):
+            for peer in others():
+                parts_copy(g, p, tensor, peer).wait_send()
+                peers_copy(g, p, tensor, peer).wait_send()
 
     @pl.when(section > 0)
     def _():
         for g in range(groups):
-            for target in replicas():
-                relay_copy(g, replica, section - 1, target).wait_send()
+            for p in range(PAIR):
+                for i, target in enumerate(targets):
+                    relay_copy(g, p, i, replica, section - 1, target).wait_send()
+
+    if bridged:
+        @pl.when((section < last) & inner)
+        def _():
+            for g in range(groups):
+                for p in range(PAIR):
+                    forward_copy(g, p, far_slot, partner).wait_send()
 
 
 def shards(out_grad, relu_mask, w_in, w_out, route):
@@ -291,10 +368,11 @@
             pltpu.VMEM((groups, n_tensor, rows, width), bf16),
             pltpu.VMEM((groups, n_replica, rows, width), bf16),
             pltpu.VMEM((groups, rows, width), bf16),
+            pltpu.VMEM((groups, rows, width), bf16),
             dma((pairs, 2)), dma((SLOTS, 2)), dma((SLOTS,)), dma((groups,)), dma((groups,)),
-            dma((groups, n_tensor)), dma((groups, n_tensor)),
-            dma((groups, n_tensor)), dma((groups, n_tensor)),
-            dma((groups, n_replica)), dma((groups, n_replica)),
+            dma((groups, PAIR, n_tensor)), dma((groups, PAIR, n_tensor)),
+            dma((groups, PAIR, n_tensor)), dma((groups, PAIR, n_tensor)),
+            dma((groups, PAIR, n_replica)), dma((groups, PAIR, n_replica)), dma((groups, PAIR)),
         ],
         compiler_params=pltpu.CompilerParams(
             collective_id=0, has_side_effects=True, vmem_limit_bytes=67043328

time: 270 us -> 252 us (0.933); the launches traced: 266 us -> 252 us
  Pallas kernels: 262 us -> 249 us
    pallas_call x1, Pallas kernels: 262 us -> 249 us  [shards(): pl.pallas_call(functools.partial(relay_kernel, sizes), out_shape=jax.Shap...]
where the time goes in v1:
time: 252 us
  Pallas kernels  249 us (99%)
  local copies, waits for them, and re-layouts  3.64 us (1%)
    pallas_call x1, Pallas kernels, shards(): pl.pallas_call(functools.partial(relay_kernel, sizes), out_shape=jax.Shap...  249 us

profile of v1, /device:TPU:0, one launch (start us, length us, event | category | flops | bytes accessed | tf_op | source)
XLA Modules:
  0.0 252.2 jit_solution(18282523557377170620)
XLA Ops:
  0.0 1.4 copy.6.route_ref
  1.4 248.5 %relay.1 = bf16[4,128,1024]{2,1,0:T(8,128)(2,1)} custom-call(s32[3,8,4]{2,1,0:T(8,128)} %copy.6.route_ref, bf16[4,128,1024]{2,1,0:T(8,128)(2,1)} %bitcast.9, s32[8,128,2048]{2,1,0:T(8,128)} %bitcast.7, bf16[1024,16384]{1,0:T(8,128)(2,1)} %bitcast.5, bf16[16384,1024]{1,0:T(8,128)(2,1)} %bitcast.6), custom_call_target="tpu_custom_call" | custom-call | tf_op jit(solution)/shard_map/relay/pallas_call | solution.py:350
  249.9 2.3 copy.8
